TPU v7x, 512 devices: a whole 4x4x16 slice. The times are simulated.
512 devices in a mesh: var: 128 (over y, x, z_lo, core), samp: 4 (over z_hi).
Axes of the slice: x: 4, y: 4, z: 16 (z_hi: 4, z_lo: 4; z = z_hi * 4 + z_lo), core: 2. Of those that a mesh axis runs over, the one named last changes fastest.
Arguments:
- dosages: int32 [1024, 131072], P('samp', 'var'), may hold values from 0 to 3, as said below
- weights: bfloat16 [131072, 2560], P(('var', 'samp')), may hold values from -0.0625 to 0.0625
- variant_pass: int32 [131072], P('var'), may hold values 0 or 1
- ancestry: float32 [1024, 20], P('samp')
Outputs:
- standardized: float32 [2560, 1024], P('var', 'samp')
Inputs may be any that keep to these rules, and one draw needn't show every extreme that they name: 3 marks a missing call; other values are allele dosages.
All inputs are finite; a program needn't handle non-finite values. No bound on the sum of `variant_pass` on one device may be relied on, other than what follows from the above.
Results may differ from a plain program's by a relative error of at most 0.0024.
Values may be sent and summed in bfloat16 or wider, within the bound.
A program may use at most 64 MiB of HBM per device.

v0:
```python
import jax
import jax.numpy as jnp
from jax import lax
from jax.sharding import PartitionSpec as P


def cholesky_apply(gram, cross):
    factor = jnp.linalg.cholesky(gram)
    order_n = gram.shape[0]
    forward = []
    for row_idx in range(order_n):
        running = cross[:, row_idx]
        for col_idx in range(row_idx):
            running = running - factor[row_idx, col_idx] * forward[col_idx]
        forward.append(running / factor[row_idx, row_idx])
    solved = [None] * order_n
    for row_idx in reversed(range(order_n)):
        running = forward[row_idx]
        for col_idx in range(row_idx + 1, order_n):
            running = running - factor[col_idx, row_idx] * solved[col_idx]
        solved[row_idx] = running / factor[row_idx, row_idx]
    return jnp.stack(solved, axis=1)


def on_device(dosages, weights, variant_pass, ancestry):
    samples_here = dosages.shape[0]
    total_samples = samples_here * lax.axis_size("samp")
    observed = dosages < 3
    allele_total, observed_count = lax.psum(
        (
            jnp.sum(jnp.where(observed, dosages, 0).astype(jnp.float32), axis=0),
            jnp.sum(observed.astype(jnp.float32), axis=0),
        ),
        "samp",
    )
    impute = ((allele_total + 1.0) / (observed_count + 1.0)).astype(jnp.bfloat16)
    genotypes = jnp.where(observed, dosages.astype(jnp.bfloat16), impute[None, :])
    genotypes = genotypes * variant_pass.astype(jnp.bfloat16)[None, :]
    full_weights = lax.all_gather(weights, "samp", axis=0, tiled=True)
    every_score = lax.dot_general(
        full_weights, genotypes, (((0,), (1,)), ((), ())), preferred_element_type=jnp.float32
    )
    raw_scores = lax.psum_scatter(every_score, "var", scatter_dimension=0, tiled=True)
    design = jnp.concatenate([jnp.ones((samples_here, 1), jnp.float32), ancestry], axis=1)
    local_gram = jnp.dot(design.T, design, precision=lax.Precision.HIGHEST)
    local_cross = jnp.dot(raw_scores, design, precision=lax.Precision.HIGHEST)
    gram = lax.psum(local_gram, "samp")
    cross = lax.psum(local_cross, "samp")
    coeffs = cholesky_apply(gram, cross)
    residual = raw_scores - jnp.dot(coeffs, design.T, precision=lax.Precision.HIGHEST)
    squared = lax.psum(jnp.sum(residual * residual, axis=1), "samp")
    spread = squared / (total_samples - 1)
    return residual / jnp.sqrt(spread + 1e-06)[:, None]


def solution(mesh):
    in_specs = (P("samp", "var"), P(("var", "samp"), None), P("var"), P("samp", None))
    out_specs = P("var", "samp")
    return jax.shard_map(
        on_device, mesh=mesh, in_specs=in_specs, out_specs=out_specs, check_vma=False
    )
```

profile of v0, /device:TPU:128, one launch (start us, length us, event | category | flops | bytes accessed | tf_op | source)
XLA Modules:
  0.0 2035.9 jit_solution(5791186550489858896)
XLA Ops:
  8.0 1.4 convert_reduce_fusion.1
  9.4 17.7 all-reduce.3
  27.2 180.4 %all-gather.2.cloned.1.call-done = bf16[1024,2560]{1,0:T(8,128)(2,1)} async-done(((bf16[256,2560]{1,0:T(8,128)(2,1)}), bf16[1024,2560]{1,0:T(8,128)(2,1)}) %all-gather.2.cloned.1.call-update) | async-done | bytes 5242896 | tf_op jit(solution)/shard_map/all_gather | solution.py:39
  207.6 6.2 convolution_bitcast_fusion
  213.8 1.3 dynamic-slice
  215.9 1290.2 %all-reduce.6.cloned.1.call-done = f32[2560,256]{0,1:T(8,128)} async-done(((f32[2560,256]{0,1:T(8,128)}), f32[2560,256]{0,1:T(8,128)}) %all-reduce.6.cloned.1.call-update) | async-done | bytes 2621456
  1506.1 1.0 constant_dynamic-slice_fusion
  1507.3 22.7 %all-reduce.2 = (f32[20,21]{0,1:T(8,128)S(1)}, f32[21,21]{0,1:T(8,128)S(1)}) all-reduce(f32[20,21]{0,1:T(8,128)S(1)} %fusion.8, f32[21,21]{0,1:T(8,128)S(1)} %fusion.6), channel_id=1, replica_groups=mesh['var'=128,'samp'=4] {'samp'}, use_global_device_ids=true, to_apply=%region_5.6 | all-reduce | flops 861 | bytes 6888 | tf_op jit(solution)/shard_map/psum | solution.py:48
  1530.1 1.9 cholesky.18
  1533.4 0.7 fusion.84
  1534.1 0.7 fusion.83
  1535.5 0.7 fusion.90
  1536.2 0.7 fusion.91
  1537.0 0.7 fusion.89
  1537.7 0.7 fusion.81
  1539.2 0.7 fusion.85
  1539.9 0.7 fusion.87
  1542.0 0.7 fusion.80
  1544.0 131.0 %subtract_divide_fusion.13 = (f32[20,1]{0,1:T(1,128)S(1)}, f32[20,1]{0,1:T(1,128)S(1)}, f32[20,1]{0,1:T(1,128)S(1)}, f32[20,1]{0,1:T(1,128)S(1)}, f32[20,1]{0,1:...) fusion(f32[20,21]{0,1:T(8,128)S(1)} %get-tuple-element.7, ...), kind=kLoop, calls=%fused_computation.141 | loop fusion | flops 8000 | bytes 4040 | tf_op jit(solution)/shard_map/div | solution.py:15
  1675.0 130.2 %subtract_divide_fusion.52 = (f32[20]{0:T(128)S(1)}, f32[20]{0:T(128)S(1)}, f32[20]{0:T(128)S(1)}, f32[20]{0:T(128)S(1)}, f32[20]{0:T(128)S(1)}, /*index=5*/f32[...) fusion(f32[20,1]{0,1:T(1,128)S(1)} %get-tuple-element.43, ...), kind=kLoop, calls=%fused_computation.181 | loop fusion | flops 7980 | bytes 3956 | tf_op jit(solution)/shard_map/div | solution.py:15
  1805.3 61.1 %subtract_divide_fusion.39 = (f32[20]{0:T(128)S(1)}, f32[20]{0:T(128)S(1)}, f32[20]{0:T(128)S(1)}, f32[20]{0:T(128)S(1)}, f32[20]{0:T(128)S(1)}, /*index=5*/f32[...) fusion(f32[20]{0:T(128)S(1)} %get-tuple-element.76, ...), kind=kLoop, calls=%fused_computation.168 | loop fusion | flops 4180 | bytes 3116 | tf_op jit(solution)/shard_map/div | solution.py:21
  1866.4 87.1 %divide_bitcast_fusion = (f32[20,1]{0,1:T(1,128)S(1)}, f32[20]{0:T(128)S(1)}, f32[20]{0:T(128)S(1)}, f32[20]{0:T(128)S(1)}, f32[20]{0:T(128)S(1)}, /*index=5*/f32[20]{0:T(128)S(1)}, f32[20]{0:T(128)S(1)}, f32[20]{0:T(128)S(1)}) fusion(f32[20]{0:T(128)S(1)} %get-tuple-element.64, f32[20]{0:T(128)S(1)} %get-tuple-element.63, f32[20]{0:T(128)S(1)} %get-tuple-element.62, ...), kind=kLoop, calls=%fused_computation.160 | loop fusion | flops 5440 | bytes 2880 | tf_op jit(solution)/shard_map/stack | solution.py:22
  1953.5 61.1 %subtract_divide_fusion = (f32[20,1]{0,1:T(1,128)S(1)}, f32[20,1]{0,1:T(1,128)S(1)}, f32[20,1]{0,1:T(1,128)S(1)}, f32[20,1]{0,1:T(1,128)S(1)}, f32[20,1]{0,1:T(1...) fusion(f32[20,1]{0,1:T(1,128)S(1)} %get-tuple-element.35, ...), kind=kLoop, calls=%fused_computation.128 | loop fusion | flops 4180 | bytes 3116 | tf_op jit(solution)/shard_map/div | solution.py:21
  2015.0 13.4 psum.39
  (24 shorter events, 7.2 us)
Async XLA Ops:
  6.5 201.1 %all-gather.2.cloned.1.call-start = ((), (), s32[]{:S(2)}) async-start(), calls=%async_computation | async-start | bytes 6553600 | tf_op jit(solution)/shard_map/all_gather | solution.py:39
  7.3 1498.8 %all-reduce.6.cloned.1.call-start = ((), (), s32[]{:S(2)}) async-start(), calls=%async_computation.1 | async-start | bytes 5242880
  213.8 2.0 copy-start
Sparse Core Ops, SparseCore 0:
  9.5 198.1 all-gather.1
  213.9 1292.0 all-reduce.5
where the time goes:
time: 2040 us
  waiting for transfers between devices  1470 us (72%)
  other arithmetic  477 us (23%)
  blocking collectives  53.8 us (3%)
    unnamed x3, waiting for transfers between devices  1290 us
    div x2, other arithmetic, cholesky_apply(): forward.append(running / factor[row_idx, row_idx])  261 us
    all_gather x1, waiting for transfers between devices, on_device(): full_weights = lax.all_gather(weights, 'samp', axis=0, tiled=True)  180 us
    div x2, other arithmetic, cholesky_apply(): solved[row_idx] = running / factor[row_idx, row_idx]  122 us
    another operation x1, other arithmetic, cholesky_apply(): return jnp.stack(solved, axis=1)  87.1 us
  transfers between devices with their start and end apart: 2, of which 2 were waited for; matrix products, arithmetic and copies ran while one was open for 0% of the time, Pallas kernels for 0%

commit v1 on v0

--- a/solution.py
+++ b/solution.py
@@ -36,7 +36,9 @@
     impute = ((allele_total + 1.0) / (observed_count + 1.0)).astype(jnp.bfloat16)
     genotypes = jnp.where(observed, dosages.astype(jnp.bfloat16), impute[None, :])
     genotypes = genotypes * variant_pass.astype(jnp.bfloat16)[None, :]
-    full_weights = lax.all_gather(weights, "samp", axis=0, tiled=True)
+    full_weights = jnp.concatenate(
+        lax.all_to_all(jnp.stack([weights] * lax.axis_size("samp")), "samp", 0, 0), axis=0
+    )
     every_score = lax.dot_general(
         full_weights, genotypes, (((0,), (1,)), ((), ())), preferred_element_type=jnp.float32
     )

time: 2040 us -> 2090 us (1.025)
  blocking collectives: 53.8 us -> 269 us
  waiting for transfers between devices: 1470 us -> 1290 us
    psum x1, blocking collectives: 17.7 us -> 233 us  [on_device(): lax.psum((jnp.sum(jnp.where(observed, dosages, 0).astype(jnp.float32), ax...]
    all_gather x1 -> x0, waiting for transfers between devices: 180 us -> none  [on_device(): full_weights = lax.all_gather(weights, 'samp', axis=0, tiled=True)]
    unnamed x3 -> x2, waiting for transfers between devices: 1290 us -> 1290 us
  transfers between devices with their start and end apart: 2 -> 2, of which waited for: 2 -> 1; matrix products, arithmetic and copies ran while one was open for 0% -> 0% of each run, Pallas kernels for 0% -> 0%
where the time goes in v1:
time: 2090 us
  waiting for transfers between devices  1290 us (62%)
  other arithmetic  475 us (23%)
  blocking collectives  269 us (13%)
    unnamed x2, waiting for transfers between devices  1290 us
    div x2, other arithmetic, cholesky_apply(): forward.append(running / factor[row_idx, row_idx])  261 us
    psum x1, blocking collectives, on_device(): lax.psum((jnp.sum(jnp.where(observed, dosages, 0).astype(jnp.float32), ax...  233 us
    div x2, other arithmetic, cholesky_apply(): solved[row_idx] = running / factor[row_idx, row_idx]  123 us
    another operation x1, other arithmetic, cholesky_apply(): return jnp.stack(solved, axis=1)  87.3 us
  transfers between devices with their start and end apart: 2, of which 1 were waited for; matrix products, arithmetic and copies ran while one was open for 0% of the time, Pallas kernels for 0%

profile of v1, /device:TPU:128, one launch (start us, length us, event | category | flops | bytes accessed | tf_op | source)
XLA Modules:
  0.0 2085.9 jit_solution(15325980164403799498)
XLA Ops:
  6.5 4.1 stack.20
  10.6 14.0 all-to-all-start
  24.8 233.1 %all-reduce.3 = (f32[1024]{0:T(1024)S(1)}, f32[1024]{0:T(1024)S(1)}) all-reduce(f32[1024]{0:T(1024)S(1)} %get-tuple-element.6, f32[1024]{0:T(1024)S(1)} %get-tuple-element.5), channel_id=1, replica_groups=mesh['var'=128,'samp'=4] {'samp'}, use_global_device_ids=true, to_apply=%region_3.4 | all-reduce | flops 2048 | bytes 16384 | tf_op jit(solution)/shard_map/psum | solution.py:29
  257.9 5.5 convolution_bitcast_fusion
  263.5 1.3 dynamic-slice
  265.6 1289.7 %all-reduce.6.cloned.1.call-done = f32[2560,256]{0,1:T(8,128)} async-done(((f32[2560,256]{0,1:T(8,128)}), f32[2560,256]{0,1:T(8,128)}) %all-reduce.6.cloned.1.call-update) | async-done | bytes 2621456
  1555.3 1.0 constant_dynamic-slice_fusion
  1556.6 22.8 %all-reduce.2 = (f32[20,21]{0,1:T(8,128)S(1)}, f32[21,21]{0,1:T(8,128)S(1)}) all-reduce(f32[20,21]{0,1:T(8,128)S(1)} %fusion.8, f32[21,21]{0,1:T(8,128)S(1)} %fusion.6), channel_id=1, replica_groups=mesh['var'=128,'samp'=4] {'samp'}, use_global_device_ids=true, to_apply=%region_5.6 | all-reduce | flops 861 | bytes 6888 | tf_op jit(solution)/shard_map/psum | solution.py:50
  1579.5 1.9 cholesky.18
  1582.8 0.7 fusion.81
  1583.5 0.7 fusion.89
  1584.2 0.7 fusion.90
  1586.3 0.7 fusion.82
  1587.1 0.7 fusion.83
  1587.8 0.7 fusion.84
  1589.2 0.7 fusion.86
  1590.0 0.7 fusion.87
  1591.4 0.7 fusion.80
  1592.1 131.1 %subtract_divide_fusion.13 = (f32[20,1]{0,1:T(1,128)S(1)}, f32[20,1]{0,1:T(1,128)S(1)}, f32[20,1]{0,1:T(1,128)S(1)}, f32[20,1]{0,1:T(1,128)S(1)}, f32[20,1]{0,1:...) fusion(f32[20,21]{0,1:T(8,128)S(1)} %get-tuple-element.7, ...), kind=kLoop, calls=%fused_computation.141 | loop fusion | flops 8000 | bytes 4040 | tf_op jit(solution)/shard_map/div | solution.py:15
  1723.2 130.3 %subtract_divide_fusion.52 = (f32[20]{0:T(128)S(1)}, f32[20]{0:T(128)S(1)}, f32[20]{0:T(128)S(1)}, f32[20]{0:T(128)S(1)}, f32[20]{0:T(128)S(1)}, /*index=5*/f32[...) fusion(f32[20,1]{0,1:T(1,128)S(1)} %get-tuple-element.43, ...), kind=kLoop, calls=%fused_computation.181 | loop fusion | flops 7980 | bytes 3956 | tf_op jit(solution)/shard_map/div | solution.py:15
  1854.9 61.3 %subtract_divide_fusion.39 = (f32[20]{0:T(128)S(1)}, f32[20]{0:T(128)S(1)}, f32[20]{0:T(128)S(1)}, f32[20]{0:T(128)S(1)}, f32[20]{0:T(128)S(1)}, /*index=5*/f32[...) fusion(f32[20]{0:T(128)S(1)} %get-tuple-element.76, ...), kind=kLoop, calls=%fused_computation.168 | loop fusion | flops 4180 | bytes 3116 | tf_op jit(solution)/shard_map/div | solution.py:21
  1916.2 87.3 %divide_bitcast_fusion = (f32[20,1]{0,1:T(1,128)S(1)}, f32[20]{0:T(128)S(1)}, f32[20]{0:T(128)S(1)}, f32[20]{0:T(128)S(1)}, f32[20]{0:T(128)S(1)}, /*index=5*/f32[20]{0:T(128)S(1)}, f32[20]{0:T(128)S(1)}, f32[20]{0:T(128)S(1)}) fusion(f32[20]{0:T(128)S(1)} %get-tuple-element.64, f32[20]{0:T(128)S(1)} %get-tuple-element.63, f32[20]{0:T(128)S(1)} %get-tuple-element.62, ...), kind=kLoop, calls=%fused_computation.160 | loop fusion | flops 5440 | bytes 2880 | tf_op jit(solution)/shard_map/stack | solution.py:22
  2003.4 61.3 %subtract_divide_fusion = (f32[20,1]{0,1:T(1,128)S(1)}, f32[20,1]{0,1:T(1,128)S(1)}, f32[20,1]{0,1:T(1,128)S(1)}, f32[20,1]{0,1:T(1,128)S(1)}, f32[20,1]{0,1:T(1...) fusion(f32[20,1]{0,1:T(1,128)S(1)} %get-tuple-element.35, ...), kind=kLoop, calls=%fused_computation.128 | loop fusion | flops 4180 | bytes 3116 | tf_op jit(solution)/shard_map/div | solution.py:21
  2065.1 13.3 psum.39
  (28 shorter events, 6.0 us)
Async XLA Ops:
  10.6 14.0 copy-start.2
  10.6 14.0 copy-start
  10.6 247.3 %all-to-all-start = ((bf16[4,256,2560]{2,1,0:T(8,128)(2,1)}), bf16[4,256,2560]{2,1,0:T(8,128)(2,1)}, u32[]{:S(2)}, u32[]{:S(2)}) async-start(bf16[4,256,2560]{2,1,0:T(8,128)(2,1)} %stack.20), calls=%async_computation | async-start | bytes 10485760 | tf_op jit(solution)/shard_map/all_to_all | solution.py:40
  24.6 1530.8 %all-reduce.6.cloned.1.call-start = ((), (), s32[]{:S(2)}) async-start(), calls=%async_computation.1 | async-start | bytes 5242880
  257.9 7.5 copy-start.1
Sparse Core Ops, SparseCore 0:
  263.6 1291.6 all-reduce.5
